TPU v7x, 128 devices: a whole 4x4x4 slice. The times are simulated.
128 devices in a mesh: req: 8 (over x_lo, y), grp: 16 (over z, x_hi, core).
Axes of the slice: x: 4 (x_hi: 2, x_lo: 2; x = x_hi * 2 + x_lo), y: 4, z: 4, core: 2. Of those that a mesh axis runs over, the one named last changes fastest.
Arguments:
- residual: bfloat16 [8, 16, 128, 4096], P('req', 'grp'), may hold values from -64 to 64
- suffix_proj: bfloat16 [8, 16, 3, 128, 4096], P('req', 'grp'), may hold values from -256 to 256
- prefix_cache: bfloat16 [8, 16, 2, 128, 4096], P('req', 'grp'), may hold values from -8 to 8
- owner_req: int32 [16], replicated, may hold values from 0 to 7, as said below
- lengths: int32 [8, 16], P('req', 'grp'), may hold values from 8 to 128, as said below
- norm_gain: float32 [4096], replicated, may hold values from 0.1 to 1.9
- up_weight: bfloat16 [12288, 4096], P('grp'), may hold values from -0.09375 to 0.09375
- down_weight: bfloat16 [12288, 4096], P('grp'), may hold values from -0.0546875 to 0.0546875
Outputs:
- output: bfloat16 [8, 16, 128, 4096], P('req', 'grp')
Inputs may be any that keep to these rules, and one draw needn't show every extreme that they name: owner_req[g] is the req index whose cache block holds group g's prefix. The first lengths[r, g] of the 128 slots of a request are live; in every req index one request fills all 128 slots.
All inputs are finite; a program needn't handle non-finite values.
Results may differ from a plain program's by a relative error of at most 0.014.
Values may be sent and summed in bfloat16 or wider, within the bound.
No kernel may reach another device: no remote copies, remote signals or barrier semaphores. Data moves between devices by JAX's collectives and lax.ppermute only.
A program may use at most 128 MiB of HBM per device.

v0:
```python
import math
import jax
import jax.numpy as jnp
from jax import lax
from jax.sharding import PartitionSpec as P

HEADS = 32
NORM_EPS = 1e-05


def from_root(value, axis, source):
    kept = jnp.where(lax.axis_index(axis) == source, value, 0).astype(value.dtype)
    return lax.psum(kept, axis)


def head_slopes(head_count):
    return jnp.exp2(-8.0 * jnp.arange(1, head_count + 1, dtype=jnp.float32) / head_count)


def attend(queries, key_rows, value_rows, key_pos, query_pos, causal):
    head_size = queries.shape[2]
    scores = jnp.einsum("qhe,khe->hqk", queries, key_rows, preferred_element_type=jnp.float32)
    scores = scores * (1.0 / math.sqrt(head_size))
    offsets = (key_pos[None, :] - query_pos[:, None]).astype(jnp.float32)
    scores = scores + head_slopes(queries.shape[1])[:, None, None] * offsets[None, :, :]
    if causal:
        scores = jnp.where((key_pos[None, :] <= query_pos[:, None])[None], scores, -jnp.inf)
    row_max = jnp.max(scores, axis=2)
    weights = jnp.exp(scores - row_max[:, :, None])
    row_total = jnp.sum(weights, axis=2)
    context = jnp.einsum(
        "hqk,khe->qhe", weights.astype(jnp.bfloat16), value_rows, preferred_element_type=jnp.float32
    )
    return (row_max, row_total, context)


def merge_parts(first, second):
    joint_max = jnp.maximum(first[0], second[0])
    first_scale = jnp.exp(first[0] - joint_max)
    second_scale = jnp.exp(second[0] - joint_max)
    numer = first[2] * first_scale.T[:, :, None] + second[2] * second_scale.T[:, :, None]
    denom = first[1] * first_scale + second[1] * second_scale
    merged = numer / denom.T[:, :, None]
    return merged.reshape(merged.shape[0], merged.shape[1] * merged.shape[2])


def layer_norm(state, norm_gain):
    values = state.astype(jnp.float32)
    center = values - jnp.mean(values, axis=-1, keepdims=True)
    spread = jnp.mean(center * center, axis=-1, keepdims=True)
    return (center * lax.rsqrt(spread + NORM_EPS) * norm_gain).astype(jnp.bfloat16)


def body(
    residual, suffix_proj, prefix_cache, owner_req, lengths, norm_gain, up_weight, down_weight
):
    slot_count = residual.shape[2]
    feature_count = residual.shape[3]
    prefix_count = prefix_cache.shape[3]
    head_count = HEADS
    head_size = feature_count // head_count
    block = suffix_proj[0, 0].reshape(3, slot_count, head_count, head_size)
    query_pos = prefix_count + jnp.arange(slot_count, dtype=jnp.int32)
    prefix_pos = jnp.arange(prefix_count, dtype=jnp.int32)
    group_index = lax.axis_index("grp")
    owner_index = lax.dynamic_index_in_dim(owner_req, group_index, 0, keepdims=False)
    cached = from_root(prefix_cache[0, 0], "req", owner_index)
    cached = cached.reshape(2, prefix_count, head_count, head_size)
    first = attend(block[0], cached[0], cached[1], prefix_pos, query_pos, False)
    second = attend(block[0], block[1], block[2], query_pos, query_pos, True)
    context = merge_parts(first, second)
    states = (residual[0, 0].astype(jnp.float32) + context).astype(jnp.bfloat16)
    normed = layer_norm(states, norm_gain)
    preactivation = lax.dot_general(
        lax.all_gather(normed, "grp", axis=0, tiled=True),
        up_weight,
        (((1,), (1,)), ((), ())),
        preferred_element_type=jnp.float32,
    )
    hidden = jax.nn.gelu(preactivation, approximate=False).astype(jnp.bfloat16)
    partial_term = jnp.dot(hidden, down_weight, preferred_element_type=jnp.float32).astype(
        jnp.bfloat16
    )
    mlp_sum = lax.psum_scatter(
        lax.optimization_barrier(partial_term).astype(jnp.float32).astype(jnp.bfloat16),
        "grp",
        scatter_dimension=0,
        tiled=True,
    ).astype(jnp.float32)
    live = jnp.arange(slot_count, dtype=jnp.int32) < lengths[0, 0]
    combined = states.astype(jnp.float32) + mlp_sum
    output = jnp.where(live[:, None], combined, 0.0).astype(jnp.bfloat16)
    return output[None, None]


def solution(mesh):
    placed = (
        P("req", "grp", None, None),
        P("req", "grp", None, None, None),
        P("req", "grp", None, None, None),
        P(),
        P("req", "grp"),
        P(),
        P("grp", None),
        P("grp", None),
    )
    return jax.shard_map(
        body, mesh=mesh, in_specs=placed, out_specs=P("req", "grp", None, None), check_vma=False
    )
```

profile of v0, /device:TPU:0, one launch (start us, length us, event | category | flops | bytes accessed | tf_op | source)
XLA Modules:
  0.0 429.7 jit_solution(6529954950171514383)
XLA Ops:
  6.5 0.0 all-reduce.2.cloned.1.call-start
  6.5 3.1 copy.16
  9.7 1.2 dynamic_slice.4
  11.6 1.4 select_bitcast_fusion
  13.0 0.0 all-reduce.2.cloned.1.call-update
  13.0 0.0 copy-start.2
  13.1 0.0 all-gather.2.cloned.1.call-start
  13.1 3.5 fusion.96
  16.7 1.6 copy.35
  18.3 2.3 copy.36
  20.6 1.3 copy.25
  21.9 0.0 copy-done.2
  21.9 1.6 copy.28
  23.5 0.1 broadcast_compare_fusion
  23.6 0.1 subtract_convert_fusion
  23.7 3.4 fusion.99
  27.1 70.7 %all-reduce.2.cloned.1.call-done = bf16[2,128,4096]{1,2,0:T(8,128)(2,1)} async-done(((bf16[2,128,4096]{1,2,0:T(8,128)(2,1)}), bf16[2,128,4096]{1,2,0:T(8,128)(2,1)}) %all-reduce.2.cloned.1.call-update) | async-done | bytes 2097168 | tf_op jit(solution)/shard_map/psum | solution.py:13
  97.9 0.0 copy-start.5
  97.9 1.8 fusion.97
  99.7 0.0 copy-start.4
  99.7 0.0 copy-start.6
  99.7 0.7 fusion.98
  100.5 0.5 fusion.56
  100.9 0.0 copy-done.5
  100.9 1.0 fusion.51
  102.0 0.0 copy-done.4
  102.0 0.0 copy-done.6
  102.0 0.0 copy-start.7
  102.0 2.5 convert_reduce_fusion
  104.6 1.9 copy.27
  106.5 0.0 copy-start
  106.5 2.5 fusion.47
  109.1 0.0 copy-done.7
  109.1 1.4 fusion.43
  110.5 0.0 all-gather.2.cloned.1.call-update
  110.5 0.2 reduce-scatter.2.cloned.1.call-start
  110.7 109.1 %all-gather.2.cloned.1.call-done = bf16[2048,4096]{1,0:T(8,128)(2,1)} async-done(((bf16[128,4096]{1,0:T(8,128)(2,1)}), bf16[2048,4096]{1,0:T(8,128)(2,1)}) %all-gather.2.cloned.1.call-update) | async-done | bytes 16777232 | tf_op jit(solution)/shard_map/all_gather | solution.py:75
  219.8 55.8 %convolution_convert_fusion = bf16[2048,4096]{1,0:T(8,128)(2,1)} fusion(bf16[768,4096]{1,0:T(8,128)(2,1)} %param.15, bf16[2048,4096]{1,0:T(8,128)(2,1)} %all-gather.2.cloned.1.call-done, bf16[768,4096]{1,0:T(8,128)(2,1)} %param.14), kind=kOutput, calls=%fused_computation | convolution fusion | flops 25880428544 | bytes 46137344 | tf_op jit(solution)/shard_map/dot_general | solution.py:81
  275.6 0.0 copy-done
  275.6 0.0 copy-start.1
  275.6 0.0 copy-start.3
  275.6 0.0 reduce-scatter.2.cloned.1.call-update
  276.5 144.0 %reduce-scatter.2.cloned.1.call-done = bf16[128,4096]{1,0:T(8,128)(2,1)} async-done(((bf16[2048,4096]{1,0:T(8,128)(2,1)}), bf16[128,4096]{1,0:T(8,128)(2,1)}) %reduce-scatter.2.cloned.1.call-update) | async-done | bytes 1048592 | tf_op jit(solution)/shard_map/reduce_scatter | solution.py:84
  420.5 0.0 copy-done.1
  420.5 0.0 copy-done.3
  420.5 2.6 fusion.58
  (6 shorter events, 0.1 us)
Async XLA Ops:
  6.5 91.3 %all-reduce.2.cloned.1.call-start = ((), (), s32[]{:S(2)}) async-start(), calls=%async_computation.1 | async-start | bytes 4194304 | tf_op jit(solution)/shard_map/psum | solution.py:13
  13.0 8.8 %copy-start.2 = (bf16[1,1,128,4096]{3,2,1,0:T(8,128)(2,1)S(1)}, bf16[1,1,128,4096]{3,2,1,0:T(8,128)(2,1)}, u32[]{:S(2)}) copy-start(bf16[1,1,128,4096]{3,2,1,0:T(8,128)(2,1)} %param.8) | copy-start | bytes 3145732
  13.1 206.8 %all-gather.2.cloned.1.call-start = ((), (), s32[]{:S(2)}) async-start(), calls=%async_computation.2 | async-start | bytes 17825792 | tf_op jit(solution)/shard_map/all_gather | solution.py:75
  97.9 3.1 copy-start.5
  99.7 2.3 copy-start.4
  99.7 2.3 copy-start.6
  102.0 7.0 %copy-start.7 = (f32[4096]{0:T(1024)S(1)}, f32[4096]{0:T(1024)}, u32[]{:S(2)}) copy-start(f32[4096]{0:T(1024)} %param.13) | copy-start | bytes 49156
  106.5 169.2 %copy-start = (f32[128,4096]{1,0:T(8,128)}, f32[128,4096]{1,0:T(8,128)S(1)}, u32[]{:S(2)}) copy-start(f32[128,4096]{1,0:T(8,128)S(1)} %copy.27) | copy-start | bytes 6291460
  110.5 310.0 %reduce-scatter.2.cloned.1.call-start = ((), (), s32[]{:S(2)}) async-start(), calls=%async_computation.3 | async-start | bytes 17825792 | tf_op jit(solution)/shard_map/reduce_scatter | solution.py:84
  275.6 144.9 %copy-start.1 = (f32[128,4096]{1,0:T(8,128)S(1)}, f32[128,4096]{1,0:T(8,128)}, u32[]{:S(2)}) copy-start(f32[128,4096]{1,0:T(8,128)} %copy-done) | copy-start | bytes 6291460
  275.6 144.9 %copy-start.3 = (bf16[1,1,128,4096]{3,2,1,0:T(8,128)(2,1)S(1)}, bf16[1,1,128,4096]{3,2,1,0:T(8,128)(2,1)}, u32[]{:S(2)}) copy-start(bf16[1,1,128,4096]{3,2,1,0:T(8,128)(2,1)} %param.8) | copy-start | bytes 3145732
Sparse Core Ops, SparseCore 0:
  13.2 84.6 all-reduce.1
  110.6 109.1 all-gather.1
  275.8 144.6 reduce-scatter.1
where the time goes:
time: 430 us
  waiting for transfers between devices  324 us (75%)
  matrix products  63 us (15%)
  local copies, waits for them, and re-layouts  18.5 us (4%)
  between operations  14.7 us (3%)
  other arithmetic  9.27 us (2%)
    reduce_scatter x1, waiting for transfers between devices, body(): lax.psum_scatter(lax.optimization_barrier(partial_term).astype(jnp.float3...  144 us
    all_gather x1, waiting for transfers between devices, body(): lax.all_gather(normed, 'grp', axis=0, tiled=True)  109 us
    psum x1, waiting for transfers between devices, from_root(): return lax.psum(kept, axis)  70.7 us
    dot_general x1, matrix products, body(): jnp.dot(hidden, down_weight, preferred_element_type=jnp.float32)  55.8 us
  transfers between devices with their start and end apart: 3, of which 3 were waited for; matrix products, arithmetic and copies ran while one was open for 3% of the time, Pallas kernels for 0%

commit v1 on v0

--- a/solution.py
+++ b/solution.py
@@ -6,6 +6,11 @@
 
 HEADS = 32
 NORM_EPS = 1e-05
+
+
+def gather_over(x, axis, dim):
+    sent = jnp.stack([x] * lax.axis_size(axis))
+    return jnp.concatenate(lax.all_to_all(sent, axis, 0, 0), axis=dim)
 
 
 def from_root(value, axis, source):
@@ -72,7 +77,7 @@
     states = (residual[0, 0].astype(jnp.float32) + context).astype(jnp.bfloat16)
     normed = layer_norm(states, norm_gain)
     preactivation = lax.dot_general(
-        lax.all_gather(normed, "grp", axis=0, tiled=True),
+        gather_over(normed, "grp", 0),
         up_weight,
         (((1,), (1,)), ((), ())),
         preferred_element_type=jnp.float32,

time: 430 us -> 515 us (1.20)
  blocking collectives: 0 us -> 193 us
  waiting for transfers between devices: 324 us -> 215 us
    all_to_all x0 -> x1, blocking collectives: none -> 193 us  [gather_over(): return jnp.concatenate(lax.all_to_all(sent, axis, 0, 0), axis=dim)]
    all_gather x1 -> x0, waiting for transfers between devices: 109 us -> none  [body(): lax.all_gather(normed, 'grp', axis=0, tiled=True)]
  transfers between devices with their start and end apart: 3 -> 2, of which waited for: 3 -> 2; matrix products, arithmetic and copies ran while one was open for 3% -> 3% of each run, Pallas kernels for 0% -> 0%
where the time goes in v1:
time: 515 us
  waiting for transfers between devices  215 us (42%)
  blocking collectives  193 us (37%)
  matrix products  63 us (12%)
  local copies, waits for them, and re-layouts  20.6 us (4%)
  between operations  15 us (3%)
  other arithmetic  8.29 us (2%)
    all_to_all x1, blocking collectives, gather_over(): return jnp.concatenate(lax.all_to_all(sent, axis, 0, 0), axis=dim)  193 us
    reduce_scatter x1, waiting for transfers between devices, body(): lax.psum_scatter(lax.optimization_barrier(partial_term).astype(jnp.float3...  144 us
    psum x1, waiting for transfers between devices, from_root(): return lax.psum(kept, axis)  70.7 us
    dot_general x1, matrix products, body(): jnp.dot(hidden, down_weight, preferred_element_type=jnp.float32)  55.8 us
  transfers between devices with their start and end apart: 2, of which 2 were waited for; matrix products, arithmetic and copies ran while one was open for 3% of the time, Pallas kernels for 0%

profile of v1, /device:TPU:0, one launch (start us, length us, event | category | flops | bytes accessed | tf_op | source)
XLA Modules:
  0.0 514.6 jit_solution(12218217411491372346)
XLA Ops:
  6.5 0.0 all-reduce.2.cloned.1.call-start
  6.5 3.1 copy.16
  9.7 1.2 dynamic_slice.4
  11.6 1.4 select_bitcast_fusion
  13.0 0.0 all-reduce.2.cloned.1.call-update
  13.0 0.0 copy-start.2
  13.0 0.0 reduce-scatter.2.cloned.1.call-start
  13.1 3.6 fusion.96
  16.7 1.6 copy.35
  18.3 2.3 copy.36
  20.6 1.3 copy.25
  21.9 0.0 copy-done.2
  21.9 1.6 copy.28
  23.6 0.1 broadcast_compare_fusion
  23.6 0.1 subtract_convert_fusion
  23.7 3.4 fusion.99
  27.2 70.7 %all-reduce.2.cloned.1.call-done = bf16[2,128,4096]{1,2,0:T(8,128)(2,1)} async-done(((bf16[2,128,4096]{1,2,0:T(8,128)(2,1)}), bf16[2,128,4096]{1,2,0:T(8,128)(2,1)}) %all-reduce.2.cloned.1.call-update) | async-done | bytes 2097168 | tf_op jit(solution)/shard_map/psum | solution.py:18
  97.9 0.0 copy-start.5
  97.9 1.8 fusion.97
  99.7 0.0 copy-start.4
  99.7 0.0 copy-start.6
  99.7 0.7 fusion.98
  100.5 0.5 fusion.56
  100.9 0.0 copy-done.5
  100.9 1.0 fusion.51
  102.0 0.0 copy-done.4
  102.0 0.0 copy-done.6
  102.0 0.0 copy-start.7
  102.0 2.5 convert_reduce_fusion
  104.6 1.9 copy.27
  106.5 0.0 copy-start
  106.5 2.5 fusion.47
  109.1 0.0 copy-done.7
  109.1 0.4 fusion.43
  109.5 2.0 stack.2
  111.5 0.0 copy-done
  111.5 193.0 %all_to_all.5 = bf16[16,128,4096]{2,1,0:T(8,128)(2,1)} all-to-all(bf16[16,128,4096]{2,1,0:T(8,128)(2,1)S(1)} %stack.2), channel_id=1, replica_groups=mesh['req'=8,'grp'=16] {'grp'}, dimensions={0} | all-to-all | bytes 33554432 | tf_op jit(solution)/shard_map/all_to_all | solution.py:13
  304.5 55.8 %convolution_convert_fusion = bf16[2048,4096]{1,0:T(8,128)(2,1)} fusion(bf16[768,4096]{1,0:T(8,128)(2,1)} %param.15, bf16[2048,4096]{1,0:T(8,128)(2,1)} %bitcast.62, bf16[768,4096]{1,0:T(8,128)(2,1)} %param.14), kind=kOutput, calls=%fused_computation | convolution fusion | flops 25880428544 | bytes 46137344 | tf_op jit(solution)/shard_map/dot_general | solution.py:86
  360.3 0.0 copy-start.1
  360.4 0.0 copy-start.3
  360.4 0.0 reduce-scatter.2.cloned.1.call-update
  361.2 143.9 %reduce-scatter.2.cloned.1.call-done = bf16[128,4096]{1,0:T(8,128)(2,1)} async-done(((bf16[2048,4096]{1,0:T(8,128)(2,1)}), bf16[128,4096]{1,0:T(8,128)(2,1)}) %reduce-scatter.2.cloned.1.call-update) | async-done | bytes 1048592 | tf_op jit(solution)/shard_map/reduce_scatter | solution.py:89
  505.1 0.0 copy-done.1
  505.1 0.0 copy-done.3
  505.1 2.6 fusion.58
  (6 shorter events, 0.1 us)
Async XLA Ops:
  6.5 91.3 %all-reduce.2.cloned.1.call-start = ((), (), s32[]{:S(2)}) async-start(), calls=%async_computation.2 | async-start | bytes 4194304 | tf_op jit(solution)/shard_map/psum | solution.py:18
  13.0 8.9 %copy-start.2 = (bf16[1,1,128,4096]{3,2,1,0:T(8,128)(2,1)S(1)}, bf16[1,1,128,4096]{3,2,1,0:T(8,128)(2,1)}, u32[]{:S(2)}) copy-start(bf16[1,1,128,4096]{3,2,1,0:T(8,128)(2,1)} %param.8) | copy-start | bytes 3145732
  13.0 492.1 %reduce-scatter.2.cloned.1.call-start = ((), (), s32[]{:S(2)}) async-start(), calls=%async_computation.3 | async-start | bytes 17825792 | tf_op jit(solution)/shard_map/reduce_scatter | solution.py:89
  97.9 3.1 copy-start.5
  99.7 2.3 copy-start.4
  99.7 2.3 copy-start.6
  102.0 7.0 %copy-start.7 = (f32[4096]{0:T(1024)S(1)}, f32[4096]{0:T(1024)}, u32[]{:S(2)}) copy-start(f32[4096]{0:T(1024)} %param.13) | copy-start | bytes 49156
  106.5 5.0 copy-start
  360.3 144.8 %copy-start.1 = (f32[128,4096]{1,0:T(8,128)S(1)}, f32[128,4096]{1,0:T(8,128)}, u32[]{:S(2)}) copy-start(f32[128,4096]{1,0:T(8,128)} %copy-done) | copy-start | bytes 6291460
  360.4 144.8 %copy-start.3 = (bf16[1,1,128,4096]{3,2,1,0:T(8,128)(2,1)S(1)}, bf16[1,1,128,4096]{3,2,1,0:T(8,128)(2,1)}, u32[]{:S(2)}) copy-start(bf16[1,1,128,4096]{3,2,1,0:T(8,128)(2,1)} %param.8) | copy-start | bytes 3145732
Sparse Core Ops, SparseCore 0:
  13.2 84.6 all-reduce.1
  360.5 144.5 reduce-scatter.1

commit v2 on v0

--- a/solution.py
+++ b/solution.py
@@ -10,7 +10,7 @@
 
 def from_root(value, axis, source):
     kept = jnp.where(lax.axis_index(axis) == source, value, 0).astype(value.dtype)
-    return lax.psum(kept, axis)
+    return jnp.sum(lax.all_gather(kept, axis), 0)
 
 
 def head_slopes(head_count):

time: 430 us -> 528 us (1.23)
  waiting for transfers between devices: 324 us -> 411 us
  other arithmetic: 9.27 us -> 18.5 us
    all_gather x0 -> x1, waiting for transfers between devices: none -> 160 us  [from_root(): return jnp.sum(lax.all_gather(kept, axis), 0)]
    psum x1 -> x0, waiting for transfers between devices: 70.7 us -> none  [from_root(): return lax.psum(kept, axis)]
    reduce_sum x0 -> x1, other arithmetic: none -> 9.18 us  [from_root(): return jnp.sum(lax.all_gather(kept, axis), 0)]
where the time goes in v2:
time: 528 us
  waiting for transfers between devices  411 us (78%)
  matrix products  64.2 us (12%)
  local copies, waits for them, and re-layouts  18.7 us (4%)
  other arithmetic  18.5 us (4%)
  between operations  14.7 us (3%)
    all_gather x1, waiting for transfers between devices, from_root(): return jnp.sum(lax.all_gather(kept, axis), 0)  160 us
    reduce_scatter x1, waiting for transfers between devices, body(): lax.psum_scatter(lax.optimization_barrier(partial_term).astype(jnp.float3...  144 us
    all_gather x1, waiting for transfers between devices, body(): lax.all_gather(normed, 'grp', axis=0, tiled=True)  108 us
    dot_general x1, matrix products, body(): jnp.dot(hidden, down_weight, preferred_element_type=jnp.float32)  55.8 us
  transfers between devices with their start and end apart: 3, of which 3 were waited for; matrix products, arithmetic and copies ran while one was open for 3% of the time, Pallas kernels for 0%

profile of v2, /device:TPU:0, one launch (start us, length us, event | category | flops | bytes accessed | tf_op | source)
XLA Modules:
  0.0 527.7 jit_solution(11478366809439364006)
XLA Ops:
  6.5 0.0 all-gather.6.cloned.1.call-start
  6.5 1.2 dynamic_slice.4
  8.4 1.5 broadcast_select_fusion
  9.9 0.0 all-gather.6.cloned.1.call-update
  9.9 0.0 copy-start.2
  9.9 0.0 all-gather.4.cloned.1.call-start
  10.0 3.6 fusion.96
  13.6 1.6 copy.47
  15.2 0.0 copy-start.4
  15.2 2.7 copy.48
  17.9 1.3 copy.37
  19.2 0.0 copy-done.2
  19.2 1.6 copy.40
  20.8 0.1 broadcast_compare_fusion
  20.9 0.1 subtract_convert_fusion
  21.0 3.3 fusion.99
  24.3 0.0 copy-done.4
  24.3 159.9 %all-gather.6.cloned.1.call-done = bf16[8,1,2,128,4096]{4,3,2,1,0:T(8,128)(2,1)} async-done(((bf16[1,1,2,128,4096]{4,3,2,1,0:T(8,128)(2,1)}), bf16[8,1,2,128,4096]{4,3,2,1,0:T(8,128)(2,1)}) %all-gather.6.cloned.1.call-update) | async-done | bytes 16777232 | tf_op jit(solution)/shard_map/all_gather | solution.py:13
  184.2 9.2 %reduce_sum.52 = bf16[2,128,4096]{2,1,0:T(8,128)(2,1)S(1)} reduce(bf16[8,1,2,128,4096]{4,3,2,1,0:T(8,128)(2,1)} %all-gather.6.cloned.1.call-done, bf16[]{:T(256)} %constant.13.clone.1), dimensions={0,1}, to_apply=%region_0.1 | reduce | flops 7340032 | bytes 18874370 | tf_op jit(solution)/shard_map/reduce_sum | solution.py:13
  193.4 1.5 fusion.97
  194.9 1.6 copy.28
  196.5 1.6 copy.27
  198.1 0.0 copy-start.6
  198.1 0.0 copy-start.5
  198.1 0.0 copy-start.7
  198.2 2.1 fusion.98
  200.2 0.5 fusion.56
  200.7 0.0 copy-done.6
  200.7 1.0 fusion.51
  201.8 0.0 copy-done.5
  201.8 0.0 copy-done.7
  201.8 0.0 copy-start.8
  201.8 2.5 convert_reduce_fusion
  204.4 1.9 copy.39
  206.3 0.0 copy-start
  206.3 2.5 fusion.47
  208.9 0.0 copy-done.8
  208.9 1.4 fusion.43
  210.3 0.0 all-gather.4.cloned.1.call-update
  210.3 0.2 reduce-scatter.2.cloned.1.call-start
  210.5 107.6 %all-gather.4.cloned.1.call-done = bf16[2048,4096]{1,0:T(8,128)(2,1)} async-done(((bf16[128,4096]{1,0:T(8,128)(2,1)}), bf16[2048,4096]{1,0:T(8,128)(2,1)}) %all-gather.4.cloned.1.call-update) | async-done | bytes 16777232 | tf_op jit(solution)/shard_map/all_gather | solution.py:75
  318.1 55.8 %convolution_convert_fusion = bf16[2048,4096]{1,0:T(8,128)(2,1)} fusion(bf16[768,4096]{1,0:T(8,128)(2,1)} %param.15, bf16[2048,4096]{1,0:T(8,128)(2,1)} %all-gather.4.cloned.1.call-done, bf16[768,4096]{1,0:T(8,128)(2,1)} %param.14), kind=kOutput, calls=%fused_computation | convolution fusion | flops 25880428544 | bytes 46137344 | tf_op jit(solution)/shard_map/dot_general | solution.py:81
  373.9 0.0 copy-done
  373.9 0.0 reduce-scatter.2.cloned.1.call-update
  374.8 143.7 %reduce-scatter.2.cloned.1.call-done = bf16[128,4096]{1,0:T(8,128)(2,1)} async-done(((bf16[2048,4096]{1,0:T(8,128)(2,1)}), bf16[128,4096]{1,0:T(8,128)(2,1)}) %reduce-scatter.2.cloned.1.call-update) | async-done | bytes 1048592 | tf_op jit(solution)/shard_map/reduce_scatter | solution.py:84
  518.5 0.0 copy-done.1
  518.5 0.0 copy-done.3
  518.5 2.6 fusion.58
  (8 shorter events, 0.1 us)
Async XLA Ops:
  6.5 177.7 %all-gather.6.cloned.1.call-start = ((), (), s32[]{:S(2)}) async-start(), calls=%async_computation.3 | async-start | bytes 18874368 | tf_op jit(solution)/shard_map/all_gather | solution.py:13
  9.9 9.3 %copy-start.2 = (bf16[1,1,128,4096]{3,2,1,0:T(8,128)(2,1)S(1)}, bf16[1,1,128,4096]{3,2,1,0:T(8,128)(2,1)}, u32[]{:S(2)}) copy-start(bf16[1,1,128,4096]{3,2,1,0:T(8,128)(2,1)} %param.8) | copy-start | bytes 3145732
  9.9 308.2 %all-gather.4.cloned.1.call-start = ((), (), s32[]{:S(2)}) async-start(), calls=%async_computation.1 | async-start | bytes 17825792 | tf_op jit(solution)/shard_map/all_gather | solution.py:75
  15.2 9.1 %copy-start.4 = (bf16[1,1,1,128,4096]{3,4,2,1,0:T(8,128)(2,1)}, bf16[1,1,1,128,4096]{3,4,2,1,0:T(8,128)(2,1)S(1)}, u32[]{:S(2)}) copy-start(bf16[1,1,1,128,4096]{3,4,2,1,0:T(8,128)(2,1)S(1)} %copy.47) | copy-start | bytes 3145732
  198.1 2.6 copy-start.6
  198.1 3.7 copy-start.5
  198.1 3.7 copy-start.7
  201.8 7.0 %copy-start.8 = (f32[4096]{0:T(1024)S(1)}, f32[4096]{0:T(1024)}, u32[]{:S(2)}) copy-start(f32[4096]{0:T(1024)} %param.13) | copy-start | bytes 49156
  206.3 167.6 %copy-start = (f32[128,4096]{1,0:T(8,128)}, f32[128,4096]{1,0:T(8,128)S(1)}, u32[]{:S(2)}) copy-start(f32[128,4096]{1,0:T(8,128)S(1)} %copy.39) | copy-start | bytes 6291460
  210.3 308.2 %reduce-scatter.2.cloned.1.call-start = ((), (), s32[]{:S(2)}) async-start(), calls=%async_computation.2 | async-start | bytes 17825792 | tf_op jit(solution)/shard_map/reduce_scatter | solution.py:84
  373.9 144.6 %copy-start.1 = (f32[128,4096]{1,0:T(8,128)S(1)}, f32[128,4096]{1,0:T(8,128)}, u32[]{:S(2)}) copy-start(f32[128,4096]{1,0:T(8,128)} %copy-done) | copy-start | bytes 6291460
  373.9 144.6 %copy-start.3 = (bf16[1,1,128,4096]{3,2,1,0:T(8,128)(2,1)S(1)}, bf16[1,1,128,4096]{3,2,1,0:T(8,128)(2,1)}, u32[]{:S(2)}) copy-start(bf16[1,1,128,4096]{3,2,1,0:T(8,128)(2,1)} %param.8) | copy-start | bytes 3145732
Sparse Core Ops, SparseCore 0:
  10.1 174.1 all-gather.5
  210.4 107.6 all-gather.3
  374.1 144.3 reduce-scatter.1
